TPU v7x, 128 devices: a whole 4x4x4 slice. The times are simulated.
128 devices in a mesh: shot: 16 (over y, x_lo, core), brick: 8 (over z, x_hi).
Axes of the slice: x: 4 (x_hi: 2, x_lo: 2; x = x_hi * 2 + x_lo), y: 4, z: 4, core: 2. Of those that a mesh axis runs over, the one named last changes fastest.
Arguments:
- latent: bfloat16 [16, 256, 32, 128], P(None, 'brick', 'shot'), may hold values from -6 to 6
- conv_in: bfloat16 [27, 16, 16], replicated, may hold values from -0.3125 to 0.3125
- conv_out: bfloat16 [27, 2, 16], replicated, may hold values from -0.3125 to 0.3125
- source_field: float32 [16, 256, 16, 128], P('shot', 'brick'), may hold values from -6 to 6
- observed: float32 [16, 3, 2048], P('shot'), may hold values from -6 to 6
- aperture: int32 [16], P('shot'), may hold values from 0 to 16, as said below
- receivers: int32 [16, 3, 2048], P('shot'), may hold values from 0 to 255, as said below
Outputs:
- grad_latent: float32 [16, 256, 32, 128], P(None, 'brick', 'shot')
- grad_first: float32 [27, 16, 16], replicated
- grad_second: float32 [27, 2, 16], replicated
Inputs may be any that keep to these rules, and one draw needn't show every extreme that they name: Every shot's aperture lies inside the grid; some shot starts at 0 and some at 16. `receivers`: each receiver's first index is below 256, its third below 128, and its second lies inside its shot's aperture.
All inputs are finite; a program needn't handle non-finite values.
Results may differ from a plain program's by a relative error of at most 0.0023.
The roundings to bfloat16 on the way count: a program that leaves them out, or rounds other values in their place, can miss the bound.
Values may be sent and summed in bfloat16 or wider, within the bound.
No kernel may reach another device: no remote copies, remote signals or barrier semaphores. Data moves between devices by JAX's collectives and lax.ppermute only.
A program may use at most 128 MiB of HBM per device.

v0:
```python
import jax
import jax.numpy as jnp
from jax import lax
from jax.sharding import PartitionSpec as P

stencil_taps = (1225.0 / 1024.0, -245.0 / 3072.0, 49.0 / 5120.0, -5.0 / 7168.0)
misfit_weight = 16.0
wave_rim = 8


def with_halo(block, sides, width):
    for axis, dim in sides:
        count = lax.axis_size(axis)
        forward = [(i, i + 1) for i in range(count - 1)]
        backward = [(target, source) for source, target in forward]
        low = lax.ppermute(
            lax.slice_in_dim(block, block.shape[dim] - width, None, axis=dim), axis, forward
        )
        high = lax.ppermute(lax.slice_in_dim(block, 0, width, axis=dim), axis, backward)
        block = jnp.concatenate([low, block, high], axis=dim)
    return block


def take_slab(array, first_index, length, which_axis):
    return lax.slice_in_dim(array, first_index, first_index + length, axis=which_axis)


def inner_part(array, which_axis):
    for other_axis in range(3):
        if other_axis != which_axis:
            array = take_slab(array, wave_rim, array.shape[other_axis] - 2 * wave_rim, other_axis)
    return array


def face_slope(array, which_axis):
    length = array.shape[which_axis] - 2 * wave_rim
    summed = jnp.zeros_like(take_slab(array, 0, length + 8, which_axis))
    for tap_index in range(1, 5):
        upper = take_slab(array, 3 + tap_index, length + 8, which_axis)
        lower = take_slab(array, 4 - tap_index, length + 8, which_axis)
        summed = summed + stencil_taps[tap_index - 1] * (upper - lower)
    return summed


def operate(wavefield_pad, buoyancy_pad):
    summed = 0.0
    for which_axis in range(3):
        field_part = inner_part(wavefield_pad, which_axis)
        weight_part = inner_part(buoyancy_pad, which_axis)
        length = field_part.shape[which_axis] - 2 * wave_rim
        face_weight = 0.5 * (
            take_slab(weight_part, 3, length + 8, which_axis)
            + take_slab(weight_part, 4, length + 8, which_axis)
        )
        face_flux = face_weight * face_slope(field_part, which_axis)
        for tap_index in range(1, 5):
            upper = take_slab(face_flux, 4 + tap_index, length, which_axis)
            lower = take_slab(face_flux, 5 - tap_index, length, which_axis)
            summed = summed + stencil_taps[tap_index - 1] * (upper - lower)
    return summed


def buoyancy_slope(scaled_pad, wavefield_pad):
    summed = 0.0
    for which_axis in range(3):
        scaled_part = inner_part(scaled_pad, which_axis)
        length = scaled_part.shape[which_axis] - 2 * wave_rim
        face_product = -face_slope(scaled_part, which_axis) * face_slope(
            inner_part(wavefield_pad, which_axis), which_axis
        )
        summed = summed + 0.5 * (
            take_slab(face_product, 4, length, which_axis)
            + take_slab(face_product, 5, length, which_axis)
        )
    return summed


def brick_rims(stacked):
    widened = with_halo(stacked, (("brick", 1),), 8)
    return jnp.pad(widened, ((0, 0), (0, 0), (wave_rim, wave_rim), (wave_rim, wave_rim)))


def tile_rims(array):
    widened = with_halo(array, (("shot", 2), ("brick", 1)), 1)
    return jnp.pad(widened, ((0, 0), (0, 0), (0, 0), (1, 1)))


def kernel_shifts():
    listed = []
    for shift_x in range(3):
        for shift_y in range(3):
            for shift_z in range(3):
                listed.append((9 * shift_x + 3 * shift_y + shift_z, shift_x, shift_y, shift_z))
    return listed


def conv_forward(padded, weights):
    extent = [padded.shape[dim_index] - 2 for dim_index in range(1, 4)]
    summed = 0.0
    for kernel_index, shift_x, shift_y, shift_z in kernel_shifts():
        window = padded[
            :,
            shift_x : shift_x + extent[0],
            shift_y : shift_y + extent[1],
            shift_z : shift_z + extent[2],
        ]
        summed = summed + jnp.einsum(
            "oc,cxyz->oxyz", weights[kernel_index], window, preferred_element_type=jnp.float32
        )
    return summed


def conv_back(grad_pad, weights):
    extent = [grad_pad.shape[dim_index] - 2 for dim_index in range(1, 4)]
    summed = 0.0
    for kernel_index, shift_x, shift_y, shift_z in kernel_shifts():
        window = grad_pad[
            :,
            2 - shift_x : 2 - shift_x + extent[0],
            2 - shift_y : 2 - shift_y + extent[1],
            2 - shift_z : 2 - shift_z + extent[2],
        ]
        summed = summed + jnp.einsum(
            "oc,oxyz->cxyz", weights[kernel_index], window, preferred_element_type=jnp.float32
        )
    return summed


def weight_grad(grads, padded):
    extent = grads.shape[1:]
    listed = []
    for kernel_index, shift_x, shift_y, shift_z in kernel_shifts():
        window = padded[
            :,
            shift_x : shift_x + extent[0],
            shift_y : shift_y + extent[1],
            shift_z : shift_z + extent[2],
        ]
        listed.append(
            jnp.einsum("oxyz,cxyz->oc", grads, window, preferred_element_type=jnp.float32)
        )
    return jnp.stack(listed)


def per_device(latent, conv_in, conv_out, source_field, observed, aperture, receivers):
    latent_pad = tile_rims(latent)
    hidden = jnp.tanh(conv_forward(latent_pad, conv_in)).astype(jnp.bfloat16)
    hidden_pad = tile_rims(hidden)
    output = conv_forward(hidden_pad, conv_out)
    squashed = jax.nn.sigmoid(output[0])
    modulus = 0.03 + 0.09 * squashed
    bent_part = jnp.tanh(output[1])
    buoyancy = jnp.exp(0.35 * bent_part)
    column = lax.all_gather(jnp.stack([modulus, buoyancy]), "shot", axis=2, tiled=True)
    first_row = aperture[0]
    window_rows = source_field.shape[2]
    window = lax.dynamic_slice_in_dim(column, first_row, window_rows, 2)
    brick_width = latent.shape[1]
    receiver_cells = receivers[0]
    local_x = receiver_cells[0] - lax.axis_index("brick") * brick_width
    owned_here = (local_x >= 0) & (local_x < brick_width)
    cell_x = jnp.clip(local_x, 0, brick_width - 1)
    cell_y = receiver_cells[1] - first_row
    cell_z = receiver_cells[2]
    recorded = observed[0]
    source = source_field[0]
    sections = recorded.shape[0]

    def inject(values):
        return jnp.zeros(source.shape, jnp.float32).at[cell_x, cell_y, cell_z].add(values)

    fields = []
    images = []
    residuals = []
    coefficient_pad = brick_rims(window)
    modulus_pad = coefficient_pad[0]
    buoyancy_pad = coefficient_pad[1]
    modulus_window = window[0]
    earlier = jnp.zeros_like(source)
    current = source
    for section_index in range(sections):
        wavefield_pad = brick_rims(current[None])[0]
        operated = operate(wavefield_pad, buoyancy_pad)
        following = 2.0 * current - earlier + modulus_window * operated
        fields.append(wavefield_pad)
        images.append(operated)
        misfit = misfit_weight * (following[cell_x, cell_y, cell_z] - recorded[len(residuals)])
        residuals.append(jnp.where(owned_here, misfit, 0.0))
        earlier = current
        current = following
    adjoint = inject(residuals[sections - 1])
    adjoint_later = jnp.zeros_like(source)
    grad_modulus = jnp.zeros_like(source)
    grad_buoyancy = jnp.zeros_like(source)
    for section_index in reversed(range(sections)):
        scaled_pad = modulus_pad * brick_rims(adjoint[None])[0]
        grad_modulus = grad_modulus + adjoint * images[section_index]
        grad_buoyancy = grad_buoyancy + buoyancy_slope(scaled_pad, fields[section_index])
        if section_index > 0:
            earlier_adjoint = (
                inject(residuals[section_index - 1])
                + 2.0 * adjoint
                + operate(scaled_pad, buoyancy_pad)
                - adjoint_later
            )
            adjoint_later = adjoint
            adjoint = earlier_adjoint
    column_grad = lax.dynamic_update_slice_in_dim(
        jnp.zeros(column.shape, jnp.float32), jnp.stack([grad_modulus, grad_buoyancy]), first_row, 2
    )
    tile_grad = lax.psum_scatter(column_grad, "shot", scatter_dimension=2, tiled=True)
    grad_output = jnp.stack(
        [
            tile_grad[0] * 0.09 * squashed * (1.0 - squashed),
            tile_grad[1] * buoyancy * 0.35 * (1.0 - bent_part * bent_part),
        ]
    ).astype(jnp.bfloat16)
    grad_hidden = conv_back(tile_rims(grad_output), conv_out)
    hidden_wide = hidden.astype(jnp.float32)
    grad_inner = (grad_hidden * (1.0 - hidden_wide * hidden_wide)).astype(jnp.bfloat16)
    grad_latent = conv_back(tile_rims(grad_inner), conv_in)
    grad_first = weight_grad(grad_inner, latent_pad)
    grad_second = weight_grad(grad_output, hidden_pad)
    grad_first, grad_second = lax.psum((grad_first, grad_second), ("shot", "brick"))
    return (grad_latent, grad_first, grad_second)


def solution(mesh):
    placed = (
        P(None, "brick", "shot", None),
        P(),
        P(),
        P("shot", "brick", None, None),
        P("shot", None, None),
        P("shot"),
        P("shot", None, None),
    )
    return jax.shard_map(
        per_device,
        mesh=mesh,
        in_specs=placed,
        out_specs=(P(None, "brick", "shot", None), P(), P()),
        check_vma=False,
    )
```

profile of v0, /device:TPU:32, one launch (start us, length us, event | category | flops | bytes accessed | tf_op | source)
XLA Modules:
  0.0 565.5 jit_solution(16717900112438961506)
XLA Ops:
  15.9 4.6 collective-permute-start.2
  20.5 3.6 collective-permute-start.3
  38.4 4.9 collective-permute-start.4
  44.8 2.0 collective-permute-done.5
  46.8 3.7 collective-permute-start.6
  50.5 4.7 collective-permute-start.7
  55.6 2.1 collective-permute-done.7
  79.7 5.9 %collective-permute-start.10 = (f32[1,8,16,128]{3,1,2,0:T(8,128)S(1)}, f32[1,8,16,128]{3,1,2,0:T(8,128)S(1)}, u32[]{:S(2)}, u32[]{:S(2)}) collective-permute-start(f32[1,8,16,128]{3,1,2,0:T(8,128)S(1)} %get-tuple-element.119), channel_id=1, source_target_pairs={{0,1},{1,2},{2,3},{3,4},{4,5},{5,6},{6,7},{8,9},{9,10},{10,11},{11... | collective-permute-start | bytes 196616 | tf_op jit(solution)/shard_map/ppermute | solution.py:16
  85.6 2.4 collective-permute-start.11
  93.2 2.2 fusion.772
  95.4 22.9 %all-gather.2.cloned.1.call-done = f32[2,32,32,128]{3,1,2,0:T(8,128)} async-done(((f32[2,32,2,128]{3,1,2,0:T(8,128)}), f32[2,32,32,128]{3,1,2,0:T(8,128)}) %all-gather.2.cloned.1.call-update) | async-done | bytes 1048592 | tf_op jit(solution)/shard_map/all_gather | solution.py:154
  119.3 4.7 collective-permute-start.8
  124.0 3.7 collective-permute-start.9
  129.3 3.4 collective-permute-done.9
  133.5 1.9 fusion.799
  135.3 2.1 fusion.802
  142.0 4.6 collective-permute-start.12
  146.7 4.0 collective-permute-start.13
  150.7 3.6 collective-permute-done.13
  161.2 4.6 collective-permute-start.14
  165.8 3.7 collective-permute-start.15
  170.7 24.9 %gather_fusion.2 = f32[2048]{0:T(1024)} fusion(f32[32,16,128]{2,0,1:T(8,128)S(1)} %get-tuple-element.78, s32[2048]{0:T(1024)S(1)} %bitcast.1233), kind=kCustom, calls=%fused_computation.2 | custom fusion | bytes 40960 | tf_op jit(solution)/shard_map/gather | solution.py:187
  195.7 25.0 %gather_fusion.1 = f32[2048]{0:T(1024)} fusion(f32[32,16,128]{2,0,1:T(8,128)S(1)} %get-tuple-element.70, s32[2048]{0:T(1024)S(1)} %bitcast.1234), kind=kCustom, calls=%fused_computation.1 | custom fusion | bytes 40960 | tf_op jit(solution)/shard_map/gather | solution.py:187
  223.7 1.8 fusion.786
  227.0 2.3 multiply_add_fusion
  229.3 16.2 %gather_fusion = f32[2048]{0:T(1024)S(1)} fusion(f32[32,16,128]{2,0,1:T(8,128)S(1)} %get-tuple-element.62, s32[2048]{0:T(1024)S(1)} %bitcast.1235), kind=kCustom, calls=%fused_computation | custom fusion | bytes 40960 | tf_op jit(solution)/shard_map/gather | solution.py:187
  245.6 11.3 %scatter_custom_fusion = f32[65536]{0:T(1024)S(1)} fusion(s32[2048]{0:T(1024)S(1)} %broadcast_select_fusion, f32[2048]{0:T(1024)S(1)} %get-tuple-element.195, f32[]{:T(128)} %constant.19.clone.1), kind=kCustom, calls=%fused_computation.892 | custom fusion | flops 2048 | bytes 262148
  257.0 3.7 collective-permute-start.16
  260.7 4.9 collective-permute-start.17
  265.6 2.9 collective-permute-done.17
  275.4 1.9 negate_multiply_fusion.1
  278.1 11.6 %scatter_fusion = f32[65536]{0:T(1024)S(1)} fusion(f32[65536]{0:T(1024)S(1)} %bitcast.1238, s32[2048]{0:T(1024)S(1)} %broadcast_select_fusion, f32[2048]{0:T(1024)S(1)} %get-tuple-element.194), kind=kCustom, calls=%fused_computation.4 | custom fusion | flops 2048 | bytes 32768
  289.9 5.2 collective-permute-start.18
  295.2 3.1 collective-permute-start.19
  298.5 4.5 collective-permute-done.19
  309.8 1.8 negate_multiply_fusion
  312.5 11.6 %scatter_fusion.1 = f32[65536]{0:T(1024)S(1)} fusion(f32[65536]{0:T(1024)S(1)} %bitcast.1244, s32[2048]{0:T(1024)S(1)} %broadcast_select_fusion, f32[2048]{0:T(1024)S(1)} %get-tuple-element.193), kind=kCustom, calls=%fused_computation.5 | custom fusion | flops 2048 | bytes 32768
  325.6 3.7 collective-permute-start.20
  329.3 4.9 collective-permute-start.21
  334.2 2.9 collective-permute-done.21
  344.9 61.2 %reduce-scatter.2.cloned.1.call-done = f32[2,32,2,128]{3,1,0,2:T(8,128)} async-done(((f32[2,32,32,128]{3,1,0,2:T(8,128)}), f32[2,32,2,128]{3,1,0,2:T(8,128)}) %reduce-scatter.2.cloned.1.call-update) | async-done | bytes 65552 | tf_op jit(solution)/shard_map/reduce_scatter | solution.py:211
  418.8 4.6 collective-permute-start.24
  423.4 3.9 collective-permute-start.25
  427.6 2.8 collective-permute-done.25
  462.4 68.7 %all-reduce.11 = (f32[27,16,16]{2,1,0:T(8,128)S(1)}, f32[27,2,16]{2,1,0:T(2,128)S(1)}) all-reduce(f32[27,16,16]{2,1,0:T(8,128)S(1)} %fusion.84, f32[27,2,16]{2,1,0:T(2,128)S(1)} %fusion.111), channel_id=1, replica_groups=mesh['shot'=16,'brick'=8] {'shot','brick'}, use_global_device_ids=true, to_apply=%region_4.5 | all-reduce | flops 7776 | bytes 62208 | tf_op jit(solution)/shard_map/psum | solution.py:224
  532.6 4.5 collective-permute-start.29
  537.2 3.1 collective-permute-start.28
  540.9 4.3 collective-permute-done.28
  (575 shorter events, 155.3 us)
Async XLA Ops:
  7.2 111.1 %all-gather.2.cloned.1.call-start = ((), (), s32[]{:S(2)}) async-start(), calls=%async_computation.1 | async-start | bytes 1114112 | tf_op jit(solution)/shard_map/all_gather | solution.py:154
  8.5 27.7 %copy-start.22 = (bf16[16,32,2,128]{3,0,2,1:T(8,128)(2,1)}, bf16[16,32,2,128]{3,0,2,1:T(8,128)(2,1)S(1)}, u32[]{:S(2)}) copy-start(bf16[16,32,2,128]{3,0,2,1:T(8,128)(2,1)S(1)} %copy.382) | copy-start | bytes 786436
  9.2 5.8 %collective-permute-start = (bf16[16,32,1,128]{3,0,2,1:T(8,128)(2,1)S(1)}, bf16[16,32,1,128]{3,0,2,1:T(8,128)(2,1)S(1)}, u32[]{:S(2)}, u32[]{:S(2)}) collective-permute-start(bf16[16,32,1,128]{3,0,2,1:T(8,128)(2,1)S(1)} %get-tuple-element.124), channel_id=1, source_target_pairs={{0,8},{8,16},{16,24},{24,32},{32,40},{40,48},{48,56},{56,64},{64,7... | collective-permute-start | bytes 393224 | tf_op jit(solution)/shard_map/ppermute | solution.py:16
  11.0 4.9 collective-permute-start.1
  15.0 29.6 %copy-start.124 = (bf16[2,16]{1,0:T(2,128)(2,1)}, bf16[2,16]{1,0:T(2,128)(2,1)S(1)}, u32[]{:S(2)}) copy-start(bf16[2,16]{1,0:T(2,128)(2,1)S(1)} %get-tuple-element.30) | copy-start | bytes 196
  15.0 40.5 %copy-start.126 = (bf16[2,16]{1,0:T(2,128)(2,1)}, bf16[2,16]{1,0:T(2,128)(2,1)S(1)}, u32[]{:S(2)}) copy-start(bf16[2,16]{1,0:T(2,128)(2,1)S(1)} %get-tuple-element.27) | copy-start | bytes 196
  15.0 52.6 %copy-start.120 = (bf16[2,16]{1,0:T(2,128)(2,1)}, bf16[2,16]{1,0:T(2,128)(2,1)S(1)}, u32[]{:S(2)}) copy-start(bf16[2,16]{1,0:T(2,128)(2,1)S(1)} %get-tuple-element.26) | copy-start | bytes 196
  15.0 52.8 %copy-start.122 = (bf16[2,16]{1,0:T(2,128)(2,1)}, bf16[2,16]{1,0:T(2,128)(2,1)S(1)}, u32[]{:S(2)}) copy-start(bf16[2,16]{1,0:T(2,128)(2,1)S(1)} %get-tuple-element.28) | copy-start | bytes 196
  15.0 20.2 %copy-start.51 = (bf16[16,32,1,128]{3,0,2,1:T(8,128)(2,1)}, bf16[16,32,1,128]{3,0,2,1:T(8,128)(2,1)S(1)}, u32[]{:S(2)}) copy-start(bf16[16,32,1,128]{3,0,2,1:T(8,128)(2,1)S(1)} %collective-permute-done) | copy-start | bytes 393220
  15.8 20.4 %copy-start.49 = (bf16[16,32,1,128]{3,0,2,1:T(8,128)(2,1)}, bf16[16,32,1,128]{3,0,2,1:T(8,128)(2,1)S(1)}, u32[]{:S(2)}) copy-start(bf16[16,32,1,128]{3,0,2,1:T(8,128)(2,1)S(1)} %collective-permute-done.1) | copy-start | bytes 393220
  15.9 15.5 %collective-permute-start.2 = (bf16[16,1,4,128]{3,0,2,1:T(8,128)(2,1)S(1)}, bf16[16,1,4,128]{3,0,2,1:T(8,128)(2,1)S(1)}, u32[]{:S(2)}, u32[]{:S(2)}) collective-permute-start(bf16[16,1,4,128]{3,0,2,1:T(8,128)(2,1)S(1)} %get-tuple-element.99), channel_id=1, source_target_pairs={{0,1},{1,2},{2,3},{3,4},{4,5},{5,6},{6,7},{8,9},{9,10},{10,11},{11... | collective-permute-start | bytes 49160 | tf_op jit(solution)/shard_map/ppermute | solution.py:16
  20.5 10.9 %collective-permute-start.3 = (bf16[16,1,4,128]{3,0,2,1:T(8,128)(2,1)S(1)}, bf16[16,1,4,128]{3,0,2,1:T(8,128)(2,1)S(1)}, u32[]{:S(2)}, u32[]{:S(2)}) collective-permute-start(bf16[16,1,4,128]{3,0,2,1:T(8,128)(2,1)S(1)} %get-tuple-element.100), channel_id=1, source_target_pairs={{1,0},{2,1},{3,2},{4,3},{5,4},{6,5},{7,6},{9,8},{10,9},{11,10},{12... | collective-permute-start | bytes 49160 | tf_op jit(solution)/shard_map/ppermute | solution.py:19
  38.4 24.4 %copy-start.6 = (bf16[16,32,2,128]{3,0,2,1:T(8,128)(2,1)}, bf16[16,32,2,128]{3,0,2,1:T(8,128)(2,1)S(1)}, u32[]{:S(2)}) copy-start(bf16[16,32,2,128]{3,0,2,1:T(8,128)(2,1)S(1)} %fusion.63) | copy-start | bytes 786436
  38.4 6.4 %collective-permute-start.4 = (bf16[16,32,1,128]{3,0,2,1:T(8,128)(2,1)S(1)}, bf16[16,32,1,128]{3,0,2,1:T(8,128)(2,1)S(1)}, u32[]{:S(2)}, u32[]{:S(2)}) collective-permute-start(bf16[16,32,1,128]{3,0,2,1:T(8,128)(2,1)S(1)} %get-tuple-element.121), channel_id=1, source_target_pairs={{0,8},{8,16},{16,24},{24,32},{32,40},{40,48},{48,56},{56,64},{64,7... | collective-permute-start | bytes 393224 | tf_op jit(solution)/shard_map/ppermute | solution.py:16
  43.3 3.5 collective-permute-start.5
  44.8 17.9 %copy-start.45 = (bf16[16,32,1,128]{3,0,2,1:T(8,128)(2,1)}, bf16[16,32,1,128]{3,0,2,1:T(8,128)(2,1)S(1)}, u32[]{:S(2)}) copy-start(bf16[16,32,1,128]{3,0,2,1:T(8,128)(2,1)S(1)} %collective-permute-done.4) | copy-start | bytes 393220
  46.8 8.8 %collective-permute-start.6 = (bf16[16,1,4,128]{3,0,2,1:T(8,128)(2,1)S(1)}, bf16[16,1,4,128]{3,0,2,1:T(8,128)(2,1)S(1)}, u32[]{:S(2)}, u32[]{:S(2)}) collective-permute-start(bf16[16,1,4,128]{3,0,2,1:T(8,128)(2,1)S(1)} %get-tuple-element.97), channel_id=1, source_target_pairs={{0,1},{1,2},{2,3},{3,4},{4,5},{5,6},{6,7},{8,9},{9,10},{10,11},{11... | collective-permute-start | bytes 49160 | tf_op jit(solution)/shard_map/ppermute | solution.py:16
  50.5 7.1 %collective-permute-start.7 = (bf16[16,1,4,128]{3,0,2,1:T(8,128)(2,1)S(1)}, bf16[16,1,4,128]{3,0,2,1:T(8,128)(2,1)S(1)}, u32[]{:S(2)}, u32[]{:S(2)}) collective-permute-start(bf16[16,1,4,128]{3,0,2,1:T(8,128)(2,1)S(1)} %get-tuple-element.98), channel_id=1, source_target_pairs={{1,0},{2,1},{3,2},{4,3},{5,4},{6,5},{7,6},{9,8},{10,9},{11,10},{12... | collective-permute-start | bytes 49160 | tf_op jit(solution)/shard_map/ppermute | solution.py:19
  79.5 326.6 %reduce-scatter.2.cloned.1.call-start = ((), (), s32[]{:S(2)}) async-start(), calls=%async_computation.2 | async-start | bytes 1114112 | tf_op jit(solution)/shard_map/reduce_scatter | solution.py:211
  79.7 12.4 %collective-permute-start.10 = (f32[1,8,16,128]{3,1,2,0:T(8,128)S(1)}, f32[1,8,16,128]{3,1,2,0:T(8,128)S(1)}, u32[]{:S(2)}, u32[]{:S(2)}) collective-permute-start(f32[1,8,16,128]{3,1,2,0:T(8,128)S(1)} %get-tuple-element.119), channel_id=1, source_target_pairs={{0,1},{1,2},{2,3},{3,4},{4,5},{5,6},{6,7},{8,9},{9,10},{10,11},{11... | collective-permute-start | bytes 196616 | tf_op jit(solution)/shard_map/ppermute | solution.py:16
  85.6 7.7 %collective-permute-start.11 = (f32[1,8,16,128]{3,1,2,0:T(8,128)S(1)}, f32[1,8,16,128]{3,1,2,0:T(8,128)S(1)}, u32[]{:S(2)}, u32[]{:S(2)}) collective-permute-start(f32[1,8,16,128]{3,1,2,0:T(8,128)S(1)} %get-tuple-element.120), channel_id=1, source_target_pairs={{1,0},{2,1},{3,2},{4,3},{5,4},{6,5},{7,6},{9,8},{10,9},{11,10},{12... | collective-permute-start | bytes 196616 | tf_op jit(solution)/shard_map/ppermute | solution.py:19
  119.3 10.1 %collective-permute-start.8 = (f32[2,8,16,128]{3,1,2,0:T(8,128)S(1)}, f32[2,8,16,128]{3,1,2,0:T(8,128)S(1)}, u32[]{:S(2)}, u32[]{:S(2)}) collective-permute-start(f32[2,8,16,128]{3,1,2,0:T(8,128)S(1)} %get-tuple-element.89), channel_id=1, source_target_pairs={{0,1},{1,2},{2,3},{3,4},{4,5},{5,6},{6,7},{8,9},{9,10},{10,11},{11... | collective-permute-start | bytes 393224 | tf_op jit(solution)/shard_map/ppermute | solution.py:16
  124.0 8.7 %collective-permute-start.9 = (f32[2,8,16,128]{3,1,2,0:T(8,128)S(1)}, f32[2,8,16,128]{3,1,2,0:T(8,128)S(1)}, u32[]{:S(2)}, u32[]{:S(2)}) collective-permute-start(f32[2,8,16,128]{3,1,2,0:T(8,128)S(1)} %get-tuple-element.90), channel_id=1, source_target_pairs={{1,0},{2,1},{3,2},{4,3},{5,4},{6,5},{7,6},{9,8},{10,9},{11,10},{12... | collective-permute-start | bytes 393224 | tf_op jit(solution)/shard_map/ppermute | solution.py:19
  135.3 19.5 %copy-start.9 = (f32[32,24,128]{2,0,1:T(8,128)}, f32[32,24,128]{2,0,1:T(8,128)S(1)}, u32[]{:S(2)}) copy-start(f32[32,24,128]{2,0,1:T(8,128)S(1)} %get-tuple-element.85) | copy-start | bytes 1179652
  137.4 19.1 %copy-start.2 = (f32[32,16,136]{2,0,1:T(8,128)}, f32[32,16,136]{2,0,1:T(8,128)S(1)}, u32[]{:S(2)}) copy-start(f32[32,16,136]{2,0,1:T(8,128)S(1)} %get-tuple-element.87) | copy-start | bytes 835588
  140.7 17.7 %copy-start.13 = (f32[40,16,128]{2,0,1:T(8,128)}, f32[40,16,128]{2,0,1:T(8,128)S(1)}, u32[]{:S(2)}) copy-start(f32[40,16,128]{2,0,1:T(8,128)S(1)} %get-tuple-element.82) | copy-start | bytes 983044
  142.0 8.7 %collective-permute-start.12 = (f32[1,8,16,128]{3,1,2,0:T(8,128)S(1)}, f32[1,8,16,128]{3,1,2,0:T(8,128)S(1)}, u32[]{:S(2)}, u32[]{:S(2)}) collective-permute-start(f32[1,8,16,128]{3,1,2,0:T(8,128)S(1)} %get-tuple-element.117), channel_id=1, source_target_pairs={{0,1},{1,2},{2,3},{3,4},{4,5},{5,6},{6,7},{8,9},{9,10},{10,11},{11... | collective-permute-start | bytes 196616 | tf_op jit(solution)/shard_map/ppermute | solution.py:16
  146.7 7.7 %collective-permute-start.13 = (f32[1,8,16,128]{3,1,2,0:T(8,128)S(1)}, f32[1,8,16,128]{3,1,2,0:T(8,128)S(1)}, u32[]{:S(2)}, u32[]{:S(2)}) collective-permute-start(f32[1,8,16,128]{3,1,2,0:T(8,128)S(1)} %get-tuple-element.118), channel_id=1, source_target_pairs={{1,0},{2,1},{3,2},{4,3},{5,4},{6,5},{7,6},{9,8},{10,9},{11,10},{12... | collective-permute-start | bytes 196616 | tf_op jit(solution)/shard_map/ppermute | solution.py:19
  161.2 59.5 %collective-permute-start.14 = (f32[1,8,16,128]{3,1,2,0:T(8,128)S(1)}, f32[1,8,16,128]{3,1,2,0:T(8,128)S(1)}, u32[]{:S(2)}, u32[]{:S(2)}) collective-permute-start(f32[1,8,16,128]{3,1,2,0:T(8,128)S(1)} %get-tuple-element.115), channel_id=1, source_target_pairs={{0,1},{1,2},{2,3},{3,4},{4,5},{5,6},{6,7},{8,9},{9,10},{10,11},{11... | collective-permute-start | bytes 196616 | tf_op jit(solution)/shard_map/ppermute | solution.py:16
  165.8 54.9 %collective-permute-start.15 = (f32[1,8,16,128]{3,1,2,0:T(8,128)S(1)}, f32[1,8,16,128]{3,1,2,0:T(8,128)S(1)}, u32[]{:S(2)}, u32[]{:S(2)}) collective-permute-start(f32[1,8,16,128]{3,1,2,0:T(8,128)S(1)} %get-tuple-element.116), channel_id=1, source_target_pairs={{1,0},{2,1},{3,2},{4,3},{5,4},{6,5},{7,6},{9,8},{10,9},{11,10},{12... | collective-permute-start | bytes 196616 | tf_op jit(solution)/shard_map/ppermute | solution.py:19
  257.0 8.6 %collective-permute-start.16 = (f32[1,8,16,128]{3,1,2,0:T(8,128)S(1)}, f32[1,8,16,128]{3,1,2,0:T(8,128)S(1)}, u32[]{:S(2)}, u32[]{:S(2)}) collective-permute-start(f32[1,8,16,128]{3,1,2,0:T(8,128)S(1)} %get-tuple-element.113), channel_id=1, source_target_pairs={{0,1},{1,2},{2,3},{3,4},{4,5},{5,6},{6,7},{8,9},{9,10},{10,11},{11... | collective-permute-start | bytes 196616 | tf_op jit(solution)/shard_map/ppermute | solution.py:16
  260.7 7.8 %collective-permute-start.17 = (f32[1,8,16,128]{3,1,2,0:T(8,128)S(1)}, f32[1,8,16,128]{3,1,2,0:T(8,128)S(1)}, u32[]{:S(2)}, u32[]{:S(2)}) collective-permute-start(f32[1,8,16,128]{3,1,2,0:T(8,128)S(1)} %get-tuple-element.114), channel_id=1, source_target_pairs={{1,0},{2,1},{3,2},{4,3},{5,4},{6,5},{7,6},{9,8},{10,9},{11,10},{12... | collective-permute-start | bytes 196616 | tf_op jit(solution)/shard_map/ppermute | solution.py:19
  289.9 8.6 %collective-permute-start.18 = (f32[1,8,16,128]{3,1,2,0:T(8,128)S(1)}, f32[1,8,16,128]{3,1,2,0:T(8,128)S(1)}, u32[]{:S(2)}, u32[]{:S(2)}) collective-permute-start(f32[1,8,16,128]{3,1,2,0:T(8,128)S(1)} %get-tuple-element.111), channel_id=1, source_target_pairs={{0,1},{1,2},{2,3},{3,4},{4,5},{5,6},{6,7},{8,9},{9,10},{10,11},{11... | collective-permute-start | bytes 196616 | tf_op jit(solution)/shard_map/ppermute | solution.py:16
  295.2 7.8 %collective-permute-start.19 = (f32[1,8,16,128]{3,1,2,0:T(8,128)S(1)}, f32[1,8,16,128]{3,1,2,0:T(8,128)S(1)}, u32[]{:S(2)}, u32[]{:S(2)}) collective-permute-start(f32[1,8,16,128]{3,1,2,0:T(8,128)S(1)} %get-tuple-element.112), channel_id=1, source_target_pairs={{1,0},{2,1},{3,2},{4,3},{5,4},{6,5},{7,6},{9,8},{10,9},{11,10},{12... | collective-permute-start | bytes 196616 | tf_op jit(solution)/shard_map/ppermute | solution.py:19
  325.6 8.6 %collective-permute-start.20 = (f32[1,8,16,128]{3,1,2,0:T(8,128)S(1)}, f32[1,8,16,128]{3,1,2,0:T(8,128)S(1)}, u32[]{:S(2)}, u32[]{:S(2)}) collective-permute-start(f32[1,8,16,128]{3,1,2,0:T(8,128)S(1)} %get-tuple-element.109), channel_id=1, source_target_pairs={{0,1},{1,2},{2,3},{3,4},{4,5},{5,6},{6,7},{8,9},{9,10},{10,11},{11... | collective-permute-start | bytes 196616 | tf_op jit(solution)/shard_map/ppermute | solution.py:16
  329.3 7.8 %collective-permute-start.21 = (f32[1,8,16,128]{3,1,2,0:T(8,128)S(1)}, f32[1,8,16,128]{3,1,2,0:T(8,128)S(1)}, u32[]{:S(2)}, u32[]{:S(2)}) collective-permute-start(f32[1,8,16,128]{3,1,2,0:T(8,128)S(1)} %get-tuple-element.110), channel_id=1, source_target_pairs={{1,0},{2,1},{3,2},{4,3},{5,4},{6,5},{7,6},{9,8},{10,9},{11,10},{12... | collective-permute-start | bytes 196616 | tf_op jit(solution)/shard_map/ppermute | solution.py:19
  344.1 62.1 %copy-start.48 = (f32[2,32,2,128]{3,1,2,0:T(8,128)S(1)}, f32[2,32,2,128]{3,1,2,0:T(8,128)}, u32[]{:S(2)}) copy-start(f32[2,32,2,128]{3,1,2,0:T(8,128)} %copy-done.47) | copy-start | bytes 196612
  344.9 66.7 %copy-start.21 = (bf16[16,33,4,128]{3,0,2,1:T(8,128)(2,1)S(1)}, bf16[16,33,4,128]{3,0,2,1:T(8,128)(2,1)}, u32[]{:S(2)}) copy-start(bf16[16,33,4,128]{3,0,2,1:T(8,128)(2,1)} %copy-done.20) | copy-start | bytes 1622020
  407.0 2.6 collective-permute-start.22
  408.3 3.1 collective-permute-start.23
  418.8 8.8 %collective-permute-start.24 = (bf16[2,1,4,128]{3,1,2,0:T(2,128)(2,1)S(1)}, bf16[2,1,4,128]{3,1,2,0:T(2,128)(2,1)S(1)}, u32[]{:S(2)}, u32[]{:S(2)}) collective-permute-start(bf16[2,1,4,128]{3,1,2,0:T(2,128)(2,1)S(1)} %get-tuple-element.153), channel_id=1, source_target_pairs={{0,1},{1,2},{2,3},{3,4},{4,5},{5,6},{6,7},{8,9},{9,10},{10,11},{11... | collective-permute-start | bytes 6152 | tf_op jit(solution)/shard_map/ppermute | solution.py:16
  423.4 7.0 %collective-permute-start.25 = (bf16[2,1,4,128]{3,1,2,0:T(2,128)(2,1)S(1)}, bf16[2,1,4,128]{3,1,2,0:T(2,128)(2,1)S(1)}, u32[]{:S(2)}, u32[]{:S(2)}) collective-permute-start(bf16[2,1,4,128]{3,1,2,0:T(2,128)(2,1)S(1)} %get-tuple-element.154), channel_id=1, source_target_pairs={{1,0},{2,1},{3,2},{4,3},{5,4},{6,5},{7,6},{9,8},{10,9},{11,10},{12... | collective-permute-start | bytes 6152 | tf_op jit(solution)/shard_map/ppermute | solution.py:19
  459.2 73.4 %collective-permute-start.26 = (bf16[16,32,1,128]{3,0,2,1:T(8,128)(2,1)S(1)}, bf16[16,32,1,128]{3,0,2,1:T(8,128)(2,1)S(1)}, u32[]{:S(2)}, u32[]{:S(2)}) collective-permute-start(bf16[16,32,1,128]{3,0,2,1:T(8,128)(2,1)S(1)} %get-tuple-element.107), channel_id=1, source_target_pairs={{0,8},{8,16},{16,24},{24,32},{32,40},{40,48},{48,56},{56,64},{64,7... | collective-permute-start | bytes 393224 | tf_op jit(solution)/shard_map/ppermute | solution.py:16
  460.5 79.8 %copy-start.97 = (bf16[1,16,16]{2,1,0:T(8,128)(2,1)S(1)}, bf16[1,16,16]{2,1,0:T(8,128)(2,1)}, u32[]{:S(2)}) copy-start(bf16[1,16,16]{2,1,0:T(8,128)(2,1)} %copy-done.96) | copy-start | bytes 1540
  460.5 72.1 %collective-permute-start.27 = (bf16[16,32,1,128]{3,0,2,1:T(8,128)(2,1)S(1)}, bf16[16,32,1,128]{3,0,2,1:T(8,128)(2,1)S(1)}, u32[]{:S(2)}, u32[]{:S(2)}) collective-permute-start(bf16[16,32,1,128]{3,0,2,1:T(8,128)(2,1)S(1)} %get-tuple-element.108), channel_id=1, source_target_pairs={{8,0},{16,8},{24,16},{32,24},{40,32},{48,40},{56,48},{64,56},{72,6... | collective-permute-start | bytes 393224 | tf_op jit(solution)/shard_map/ppermute | solution.py:19
  462.4 78.2 %copy-start.99 = (bf16[1,16,16]{2,1,0:T(8,128)(2,1)S(1)}, bf16[1,16,16]{2,1,0:T(8,128)(2,1)}, u32[]{:S(2)}) copy-start(bf16[1,16,16]{2,1,0:T(8,128)(2,1)} %copy-done.98) | copy-start | bytes 1540
  532.6 8.2 %collective-permute-start.29 = (bf16[16,1,4,128]{3,0,2,1:T(8,128)(2,1)S(1)}, bf16[16,1,4,128]{3,0,2,1:T(8,128)(2,1)S(1)}, u32[]{:S(2)}, u32[]{:S(2)}) collective-permute-start(bf16[16,1,4,128]{3,0,2,1:T(8,128)(2,1)S(1)} %get-tuple-element.92), channel_id=1, source_target_pairs={{1,0},{2,1},{3,2},{4,3},{5,4},{6,5},{7,6},{9,8},{10,9},{11,10},{12... | collective-permute-start | bytes 49160 | tf_op jit(solution)/shard_map/ppermute | solution.py:19
  537.2 8.0 %collective-permute-start.28 = (bf16[16,1,4,128]{3,0,2,1:T(8,128)(2,1)S(1)}, bf16[16,1,4,128]{3,0,2,1:T(8,128)(2,1)S(1)}, u32[]{:S(2)}, u32[]{:S(2)}) collective-permute-start(bf16[16,1,4,128]{3,0,2,1:T(8,128)(2,1)S(1)} %get-tuple-element.91), channel_id=1, source_target_pairs={{0,1},{1,2},{2,3},{3,4},{4,5},{5,6},{6,7},{8,9},{9,10},{10,11},{11... | collective-permute-start | bytes 49160 | tf_op jit(solution)/shard_map/ppermute | solution.py:16
  (116 other events, 501.9 us)
Sparse Core Ops, SparseCore 0:
  79.6 38.5 all-gather.1
  345.1 61.0 reduce-scatter.1
where the time goes:
time: 575 us; the launch traced here: 566 us
  waiting for transfers between devices  116 us (20%)
  starting transfers between devices  106 us (18%)
  local copies, waits for them, and re-layouts  98.6 us (17%)
  other arithmetic  88.4 us (15%)
  matrix products  69.4 us (12%)
  blocking collectives  68.7 us (12%)
  between operations  17.5 us (3%)
    psum x1, blocking collectives, per_device(): lax.psum((grad_first, grad_second), ('shot', 'brick'))  68.7 us
    gather x3, local copies, waits for them, and re-layouts, per_device(): following[cell_x, cell_y, cell_z] - recorded[len(residuals)]  66.2 us
    reduce_scatter x1, waiting for transfers between devices, per_device(): lax.psum_scatter(column_grad, 'shot', scatter_dimension=2, tiled=True)  61.2 us
    ppermute x15, starting transfers between devices, with_halo(): lax.ppermute(lax.slice_in_dim(block, block.shape[dim] - width, None, axis...  57.8 us
    ppermute x15, starting transfers between devices, with_halo(): lax.ppermute(lax.slice_in_dim(block, 0, width, axis=dim), axis, backward)  48.6 us
    unnamed x6, other arithmetic  35.9 us
    dot_general x54, matrix products, conv_back(): jnp.einsum('oc,oxyz->cxyz', weights[kernel_index], window, preferred_elem...  29.4 us
    ppermute x15, waiting for transfers between devices, with_halo(): lax.ppermute(lax.slice_in_dim(block, 0, width, axis=dim), axis, backward)  27.5 us
  transfers between devices with their start and end apart: 32, of which 16 were waited for; matrix products, arithmetic and copies ran while one was open for 13% of the time, Pallas kernels for 0%

commit v1 on v0

--- a/solution.py
+++ b/solution.py
@@ -221,7 +221,7 @@
     grad_latent = conv_back(tile_rims(grad_inner), conv_in)
     grad_first = weight_grad(grad_inner, latent_pad)
     grad_second = weight_grad(grad_output, hidden_pad)
-    grad_first, grad_second = lax.psum((grad_first, grad_second), ("shot", "brick"))
+    grad_first, grad_second = lax.psum(lax.psum((grad_first, grad_second), "shot"), "brick")
     return (grad_latent, grad_first, grad_second)
 
 

time: 575 us -> 607 us (1.056)
  blocking collectives: 68.7 us -> 101 us
    psum x1 -> x2, blocking collectives: 68.7 us -> 101 us  [the longest x1 58.3 us: per_device(): lax.psum((grad_first, grad_second), 'shot')]
  transfers between devices with their start and end apart: 32 -> 32, of which waited for: 16 -> 16; matrix products, arithmetic and copies ran while one was open for 13% -> 12% of each run, Pallas kernels for 0% -> 0%
where the time goes in v1:
time: 607 us; the launch traced here: 596 us
  waiting for transfers between devices  115 us (19%)
  starting transfers between devices  106 us (17%)
  blocking collectives  101 us (17%)
  local copies, waits for them, and re-layouts  98.6 us (16%)
  other arithmetic  88.4 us (15%)
  matrix products  69.3 us (11%)
  between operations  17.5 us (3%)
    gather x3, local copies, waits for them, and re-layouts, per_device(): following[cell_x, cell_y, cell_z] - recorded[len(residuals)]  66.1 us
    reduce_scatter x1, waiting for transfers between devices, per_device(): lax.psum_scatter(column_grad, 'shot', scatter_dimension=2, tiled=True)  61.2 us
    ppermute x15, starting transfers between devices, with_halo(): lax.ppermute(lax.slice_in_dim(block, block.shape[dim] - width, None, axis...  59.7 us
    psum x1, blocking collectives, per_device(): lax.psum((grad_first, grad_second), 'shot')  58.3 us
    ppermute x15, starting transfers between devices, with_halo(): lax.ppermute(lax.slice_in_dim(block, 0, width, axis=dim), axis, backward)  46.8 us
    psum x1, blocking collectives, per_device(): lax.psum(lax.psum((grad_first, grad_second), 'shot'), 'brick')  42.5 us
    unnamed x6, other arithmetic  36 us
    dot_general x54, matrix products, conv_back(): jnp.einsum('oc,oxyz->cxyz', weights[kernel_index], window, preferred_elem...  29.3 us
  transfers between devices with their start and end apart: 32, of which 16 were waited for; matrix products, arithmetic and copies ran while one was open for 12% of the time, Pallas kernels for 0%

profile of v1, /device:TPU:32, one launch (start us, length us, event | category | flops | bytes accessed | tf_op | source)
XLA Modules:
  0.0 596.5 jit_solution(981671229977143499)
XLA Ops:
  15.8 4.6 collective-permute-start.2
  20.5 3.6 collective-permute-start.3
  38.4 4.9 collective-permute-start.4
  44.8 1.9 collective-permute-done.5
  46.8 3.7 collective-permute-start.6
  50.5 4.7 collective-permute-start.7
  55.6 2.1 collective-permute-done.7
  79.6 5.9 collective-permute-start.10
  85.5 2.4 collective-permute-start.11
  93.2 2.2 fusion.772
  95.4 22.9 %all-gather.2.cloned.1.call-done = f32[2,32,32,128]{3,1,2,0:T(8,128)} async-done(((f32[2,32,2,128]{3,1,2,0:T(8,128)}), f32[2,32,32,128]{3,1,2,0:T(8,128)}) %all-gather.2.cloned.1.call-update) | async-done | bytes 1048592 | tf_op jit(solution)/shard_map/all_gather | solution.py:154
  119.2 4.7 collective-permute-start.8
  124.0 3.7 collective-permute-start.9
  129.3 3.4 collective-permute-done.9
  133.4 1.9 fusion.799
  135.3 2.1 fusion.802
  142.0 4.6 collective-permute-start.12
  146.6 4.0 collective-permute-start.13
  150.7 3.6 collective-permute-done.13
  161.1 4.6 collective-permute-start.14
  165.7 3.6 collective-permute-start.15
  170.7 24.9 %gather_fusion.2 = f32[2048]{0:T(1024)} fusion(f32[32,16,128]{2,0,1:T(8,128)S(1)} %get-tuple-element.80, s32[2048]{0:T(1024)S(1)} %bitcast.1233), kind=kCustom, calls=%fused_computation.2 | custom fusion | bytes 40960 | tf_op jit(solution)/shard_map/gather | solution.py:187
  195.6 25.0 %gather_fusion.1 = f32[2048]{0:T(1024)} fusion(f32[32,16,128]{2,0,1:T(8,128)S(1)} %get-tuple-element.72, s32[2048]{0:T(1024)S(1)} %bitcast.1234), kind=kCustom, calls=%fused_computation.1 | custom fusion | bytes 40960 | tf_op jit(solution)/shard_map/gather | solution.py:187
  223.5 1.8 fusion.786
  226.9 2.3 multiply_add_fusion
  229.2 16.2 %gather_fusion = f32[2048]{0:T(1024)S(1)} fusion(f32[32,16,128]{2,0,1:T(8,128)S(1)} %get-tuple-element.64, s32[2048]{0:T(1024)S(1)} %bitcast.1235), kind=kCustom, calls=%fused_computation | custom fusion | bytes 40960 | tf_op jit(solution)/shard_map/gather | solution.py:187
  245.5 11.3 %scatter_custom_fusion = f32[65536]{0:T(1024)S(1)} fusion(s32[2048]{0:T(1024)S(1)} %broadcast_select_fusion, f32[2048]{0:T(1024)S(1)} %get-tuple-element.197, f32[]{:T(128)} %constant.19.clone.1), kind=kCustom, calls=%fused_computation.892 | custom fusion | flops 2048 | bytes 262148
  256.9 3.7 collective-permute-start.16
  260.6 4.8 collective-permute-start.17
  265.5 2.9 collective-permute-done.17
  275.3 1.8 negate_multiply_fusion.1
  278.0 11.6 %scatter_fusion = f32[65536]{0:T(1024)S(1)} fusion(f32[65536]{0:T(1024)S(1)} %bitcast.1238, s32[2048]{0:T(1024)S(1)} %broadcast_select_fusion, f32[2048]{0:T(1024)S(1)} %get-tuple-element.196), kind=kCustom, calls=%fused_computation.4 | custom fusion | flops 2048 | bytes 32768
  289.8 5.2 collective-permute-start.18
  295.0 3.1 collective-permute-start.19
  298.3 4.5 collective-permute-done.19
  312.4 11.6 %scatter_fusion.1 = f32[65536]{0:T(1024)S(1)} fusion(f32[65536]{0:T(1024)S(1)} %bitcast.1244, s32[2048]{0:T(1024)S(1)} %broadcast_select_fusion, f32[2048]{0:T(1024)S(1)} %get-tuple-element.195), kind=kCustom, calls=%fused_computation.5 | custom fusion | flops 2048 | bytes 32768
  325.4 3.7 collective-permute-start.20
  329.1 4.9 collective-permute-start.21
  334.1 2.9 collective-permute-done.21
  344.8 61.2 %reduce-scatter.2.cloned.1.call-done = f32[2,32,2,128]{3,1,0,2:T(8,128)} async-done(((f32[2,32,32,128]{3,1,0,2:T(8,128)}), f32[2,32,2,128]{3,1,0,2:T(8,128)}) %reduce-scatter.2.cloned.1.call-update) | async-done | bytes 65552 | tf_op jit(solution)/shard_map/reduce_scatter | solution.py:211
  418.7 4.6 collective-permute-start.24
  423.3 3.9 collective-permute-start.25
  427.5 2.8 collective-permute-done.25
  462.2 58.3 %all-reduce.11 = (f32[27,16,16]{2,1,0:T(8,128)S(1)}, f32[27,2,16]{2,1,0:T(2,128)S(1)}) all-reduce(f32[27,16,16]{2,1,0:T(8,128)S(1)} %fusion.84, f32[27,2,16]{2,1,0:T(2,128)S(1)} %fusion.111), channel_id=1, replica_groups=mesh['shot'=16,'brick'=8] {'shot'}, use_global_device_ids=true, to_apply=%region_4.5 | all-reduce | flops 7776 | bytes 62208 | tf_op jit(solution)/shard_map/psum | solution.py:224
  520.5 42.5 %all-reduce.12 = (f32[27,16,16]{2,1,0:T(8,128)S(1)}, f32[27,2,16]{2,1,0:T(2,128)S(1)}) all-reduce(f32[27,16,16]{2,1,0:T(8,128)S(1)} %get-tuple-element.45, f32[27,2,16]{2,1,0:T(2,128)S(1)} %get-tuple-element.46), channel_id=1, replica_groups=mesh['shot'=16,'brick'=8] {'brick'}, use_global_device_ids=true, to_apply=%region_5.6 | all-reduce | flops 7776 | bytes 62208 | tf_op jit(solution)/shard_map/psum | solution.py:224
  564.6 2.7 collective-permute-start.29
  567.2 5.0 collective-permute-start.28
  572.8 3.3 collective-permute-done.28
  (576 shorter events, 157.1 us)
Async XLA Ops:
  7.2 111.1 %all-gather.2.cloned.1.call-start = ((), (), s32[]{:S(2)}) async-start(), calls=%async_computation.1 | async-start | bytes 1114112 | tf_op jit(solution)/shard_map/all_gather | solution.py:154
  8.5 27.7 %copy-start.22 = (bf16[16,32,2,128]{3,0,2,1:T(8,128)(2,1)}, bf16[16,32,2,128]{3,0,2,1:T(8,128)(2,1)S(1)}, u32[]{:S(2)}) copy-start(bf16[16,32,2,128]{3,0,2,1:T(8,128)(2,1)S(1)} %copy.382) | copy-start | bytes 786436
  9.2 5.8 collective-permute-start
  11.0 4.9 collective-permute-start.1
  15.0 29.7 %copy-start.124 = (bf16[2,16]{1,0:T(2,128)(2,1)}, bf16[2,16]{1,0:T(2,128)(2,1)S(1)}, u32[]{:S(2)}) copy-start(bf16[2,16]{1,0:T(2,128)(2,1)S(1)} %get-tuple-element.30) | copy-start | bytes 196
  15.0 40.5 %copy-start.126 = (bf16[2,16]{1,0:T(2,128)(2,1)}, bf16[2,16]{1,0:T(2,128)(2,1)S(1)}, u32[]{:S(2)}) copy-start(bf16[2,16]{1,0:T(2,128)(2,1)S(1)} %get-tuple-element.27) | copy-start | bytes 196
  15.0 52.5 %copy-start.120 = (bf16[2,16]{1,0:T(2,128)(2,1)}, bf16[2,16]{1,0:T(2,128)(2,1)S(1)}, u32[]{:S(2)}) copy-start(bf16[2,16]{1,0:T(2,128)(2,1)S(1)} %get-tuple-element.26) | copy-start | bytes 196
  15.0 52.7 %copy-start.122 = (bf16[2,16]{1,0:T(2,128)(2,1)}, bf16[2,16]{1,0:T(2,128)(2,1)S(1)}, u32[]{:S(2)}) copy-start(bf16[2,16]{1,0:T(2,128)(2,1)S(1)} %get-tuple-element.28) | copy-start | bytes 196
  15.0 20.3 %copy-start.51 = (bf16[16,32,1,128]{3,0,2,1:T(8,128)(2,1)}, bf16[16,32,1,128]{3,0,2,1:T(8,128)(2,1)S(1)}, u32[]{:S(2)}) copy-start(bf16[16,32,1,128]{3,0,2,1:T(8,128)(2,1)S(1)} %collective-permute-done) | copy-start | bytes 393220
  15.8 20.4 %copy-start.49 = (bf16[16,32,1,128]{3,0,2,1:T(8,128)(2,1)}, bf16[16,32,1,128]{3,0,2,1:T(8,128)(2,1)S(1)}, u32[]{:S(2)}) copy-start(bf16[16,32,1,128]{3,0,2,1:T(8,128)(2,1)S(1)} %collective-permute-done.1) | copy-start | bytes 393220
  15.8 15.5 %collective-permute-start.2 = (bf16[16,1,4,128]{3,0,2,1:T(8,128)(2,1)S(1)}, bf16[16,1,4,128]{3,0,2,1:T(8,128)(2,1)S(1)}, u32[]{:S(2)}, u32[]{:S(2)}) collective-permute-start(bf16[16,1,4,128]{3,0,2,1:T(8,128)(2,1)S(1)} %get-tuple-element.101), channel_id=1, source_target_pairs={{0,1},{1,2},{2,3},{3,4},{4,5},{5,6},{6,7},{8,9},{9,10},{10,11},{11... | collective-permute-start | bytes 49160 | tf_op jit(solution)/shard_map/ppermute | solution.py:16
  20.5 10.9 %collective-permute-start.3 = (bf16[16,1,4,128]{3,0,2,1:T(8,128)(2,1)S(1)}, bf16[16,1,4,128]{3,0,2,1:T(8,128)(2,1)S(1)}, u32[]{:S(2)}, u32[]{:S(2)}) collective-permute-start(bf16[16,1,4,128]{3,0,2,1:T(8,128)(2,1)S(1)} %get-tuple-element.102), channel_id=1, source_target_pairs={{1,0},{2,1},{3,2},{4,3},{5,4},{6,5},{7,6},{9,8},{10,9},{11,10},{12... | collective-permute-start | bytes 49160 | tf_op jit(solution)/shard_map/ppermute | solution.py:19
  38.4 24.2 %copy-start.6 = (bf16[16,32,2,128]{3,0,2,1:T(8,128)(2,1)}, bf16[16,32,2,128]{3,0,2,1:T(8,128)(2,1)S(1)}, u32[]{:S(2)}) copy-start(bf16[16,32,2,128]{3,0,2,1:T(8,128)(2,1)S(1)} %fusion.63) | copy-start | bytes 786436
  38.4 6.4 %collective-permute-start.4 = (bf16[16,32,1,128]{3,0,2,1:T(8,128)(2,1)S(1)}, bf16[16,32,1,128]{3,0,2,1:T(8,128)(2,1)S(1)}, u32[]{:S(2)}, u32[]{:S(2)}) collective-permute-start(bf16[16,32,1,128]{3,0,2,1:T(8,128)(2,1)S(1)} %get-tuple-element.123), channel_id=1, source_target_pairs={{0,8},{8,16},{16,24},{24,32},{32,40},{40,48},{48,56},{56,64},{64,7... | collective-permute-start | bytes 393224 | tf_op jit(solution)/shard_map/ppermute | solution.py:16
  43.3 3.4 collective-permute-start.5
  44.8 17.8 %copy-start.45 = (bf16[16,32,1,128]{3,0,2,1:T(8,128)(2,1)}, bf16[16,32,1,128]{3,0,2,1:T(8,128)(2,1)S(1)}, u32[]{:S(2)}) copy-start(bf16[16,32,1,128]{3,0,2,1:T(8,128)(2,1)S(1)} %collective-permute-done.4) | copy-start | bytes 393220
  46.8 8.8 %collective-permute-start.6 = (bf16[16,1,4,128]{3,0,2,1:T(8,128)(2,1)S(1)}, bf16[16,1,4,128]{3,0,2,1:T(8,128)(2,1)S(1)}, u32[]{:S(2)}, u32[]{:S(2)}) collective-permute-start(bf16[16,1,4,128]{3,0,2,1:T(8,128)(2,1)S(1)} %get-tuple-element.99), channel_id=1, source_target_pairs={{0,1},{1,2},{2,3},{3,4},{4,5},{5,6},{6,7},{8,9},{9,10},{10,11},{11... | collective-permute-start | bytes 49160 | tf_op jit(solution)/shard_map/ppermute | solution.py:16
  50.5 7.1 %collective-permute-start.7 = (bf16[16,1,4,128]{3,0,2,1:T(8,128)(2,1)S(1)}, bf16[16,1,4,128]{3,0,2,1:T(8,128)(2,1)S(1)}, u32[]{:S(2)}, u32[]{:S(2)}) collective-permute-start(bf16[16,1,4,128]{3,0,2,1:T(8,128)(2,1)S(1)} %get-tuple-element.100), channel_id=1, source_target_pairs={{1,0},{2,1},{3,2},{4,3},{5,4},{6,5},{7,6},{9,8},{10,9},{11,10},{12... | collective-permute-start | bytes 49160 | tf_op jit(solution)/shard_map/ppermute | solution.py:19
  79.5 326.5 %reduce-scatter.2.cloned.1.call-start = ((), (), s32[]{:S(2)}) async-start(), calls=%async_computation.2 | async-start | bytes 1114112 | tf_op jit(solution)/shard_map/reduce_scatter | solution.py:211
  79.6 12.5 %collective-permute-start.10 = (f32[1,8,16,128]{3,1,2,0:T(8,128)S(1)}, f32[1,8,16,128]{3,1,2,0:T(8,128)S(1)}, u32[]{:S(2)}, u32[]{:S(2)}) collective-permute-start(f32[1,8,16,128]{3,1,2,0:T(8,128)S(1)} %get-tuple-element.121), channel_id=1, source_target_pairs={{0,1},{1,2},{2,3},{3,4},{4,5},{5,6},{6,7},{8,9},{9,10},{10,11},{11... | collective-permute-start | bytes 196616 | tf_op jit(solution)/shard_map/ppermute | solution.py:16
  85.5 7.7 %collective-permute-start.11 = (f32[1,8,16,128]{3,1,2,0:T(8,128)S(1)}, f32[1,8,16,128]{3,1,2,0:T(8,128)S(1)}, u32[]{:S(2)}, u32[]{:S(2)}) collective-permute-start(f32[1,8,16,128]{3,1,2,0:T(8,128)S(1)} %get-tuple-element.122), channel_id=1, source_target_pairs={{1,0},{2,1},{3,2},{4,3},{5,4},{6,5},{7,6},{9,8},{10,9},{11,10},{12... | collective-permute-start | bytes 196616 | tf_op jit(solution)/shard_map/ppermute | solution.py:19
  119.2 10.1 %collective-permute-start.8 = (f32[2,8,16,128]{3,1,2,0:T(8,128)S(1)}, f32[2,8,16,128]{3,1,2,0:T(8,128)S(1)}, u32[]{:S(2)}, u32[]{:S(2)}) collective-permute-start(f32[2,8,16,128]{3,1,2,0:T(8,128)S(1)} %get-tuple-element.91), channel_id=1, source_target_pairs={{0,1},{1,2},{2,3},{3,4},{4,5},{5,6},{6,7},{8,9},{9,10},{10,11},{11... | collective-permute-start | bytes 393224 | tf_op jit(solution)/shard_map/ppermute | solution.py:16
  124.0 8.7 %collective-permute-start.9 = (f32[2,8,16,128]{3,1,2,0:T(8,128)S(1)}, f32[2,8,16,128]{3,1,2,0:T(8,128)S(1)}, u32[]{:S(2)}, u32[]{:S(2)}) collective-permute-start(f32[2,8,16,128]{3,1,2,0:T(8,128)S(1)} %get-tuple-element.92), channel_id=1, source_target_pairs={{1,0},{2,1},{3,2},{4,3},{5,4},{6,5},{7,6},{9,8},{10,9},{11,10},{12... | collective-permute-start | bytes 393224 | tf_op jit(solution)/shard_map/ppermute | solution.py:19
  135.3 19.5 %copy-start.9 = (f32[32,24,128]{2,0,1:T(8,128)}, f32[32,24,128]{2,0,1:T(8,128)S(1)}, u32[]{:S(2)}) copy-start(f32[32,24,128]{2,0,1:T(8,128)S(1)} %get-tuple-element.87) | copy-start | bytes 1179652
  137.4 19.1 %copy-start.2 = (f32[32,16,136]{2,0,1:T(8,128)}, f32[32,16,136]{2,0,1:T(8,128)S(1)}, u32[]{:S(2)}) copy-start(f32[32,16,136]{2,0,1:T(8,128)S(1)} %get-tuple-element.89) | copy-start | bytes 835588
  140.6 17.7 %copy-start.13 = (f32[40,16,128]{2,0,1:T(8,128)}, f32[40,16,128]{2,0,1:T(8,128)S(1)}, u32[]{:S(2)}) copy-start(f32[40,16,128]{2,0,1:T(8,128)S(1)} %get-tuple-element.84) | copy-start | bytes 983044
  142.0 8.7 %collective-permute-start.12 = (f32[1,8,16,128]{3,1,2,0:T(8,128)S(1)}, f32[1,8,16,128]{3,1,2,0:T(8,128)S(1)}, u32[]{:S(2)}, u32[]{:S(2)}) collective-permute-start(f32[1,8,16,128]{3,1,2,0:T(8,128)S(1)} %get-tuple-element.119), channel_id=1, source_target_pairs={{0,1},{1,2},{2,3},{3,4},{4,5},{5,6},{6,7},{8,9},{9,10},{10,11},{11... | collective-permute-start | bytes 196616 | tf_op jit(solution)/shard_map/ppermute | solution.py:16
  146.6 7.7 %collective-permute-start.13 = (f32[1,8,16,128]{3,1,2,0:T(8,128)S(1)}, f32[1,8,16,128]{3,1,2,0:T(8,128)S(1)}, u32[]{:S(2)}, u32[]{:S(2)}) collective-permute-start(f32[1,8,16,128]{3,1,2,0:T(8,128)S(1)} %get-tuple-element.120), channel_id=1, source_target_pairs={{1,0},{2,1},{3,2},{4,3},{5,4},{6,5},{7,6},{9,8},{10,9},{11,10},{12... | collective-permute-start | bytes 196616 | tf_op jit(solution)/shard_map/ppermute | solution.py:19
  161.1 59.5 %collective-permute-start.14 = (f32[1,8,16,128]{3,1,2,0:T(8,128)S(1)}, f32[1,8,16,128]{3,1,2,0:T(8,128)S(1)}, u32[]{:S(2)}, u32[]{:S(2)}) collective-permute-start(f32[1,8,16,128]{3,1,2,0:T(8,128)S(1)} %get-tuple-element.117), channel_id=1, source_target_pairs={{0,1},{1,2},{2,3},{3,4},{4,5},{5,6},{6,7},{8,9},{9,10},{10,11},{11... | collective-permute-start | bytes 196616 | tf_op jit(solution)/shard_map/ppermute | solution.py:16
  165.7 54.8 %collective-permute-start.15 = (f32[1,8,16,128]{3,1,2,0:T(8,128)S(1)}, f32[1,8,16,128]{3,1,2,0:T(8,128)S(1)}, u32[]{:S(2)}, u32[]{:S(2)}) collective-permute-start(f32[1,8,16,128]{3,1,2,0:T(8,128)S(1)} %get-tuple-element.118), channel_id=1, source_target_pairs={{1,0},{2,1},{3,2},{4,3},{5,4},{6,5},{7,6},{9,8},{10,9},{11,10},{12... | collective-permute-start | bytes 196616 | tf_op jit(solution)/shard_map/ppermute | solution.py:19
  256.9 8.6 %collective-permute-start.16 = (f32[1,8,16,128]{3,1,2,0:T(8,128)S(1)}, f32[1,8,16,128]{3,1,2,0:T(8,128)S(1)}, u32[]{:S(2)}, u32[]{:S(2)}) collective-permute-start(f32[1,8,16,128]{3,1,2,0:T(8,128)S(1)} %get-tuple-element.115), channel_id=1, source_target_pairs={{0,1},{1,2},{2,3},{3,4},{4,5},{5,6},{6,7},{8,9},{9,10},{10,11},{11... | collective-permute-start | bytes 196616 | tf_op jit(solution)/shard_map/ppermute | solution.py:16
  260.6 7.8 %collective-permute-start.17 = (f32[1,8,16,128]{3,1,2,0:T(8,128)S(1)}, f32[1,8,16,128]{3,1,2,0:T(8,128)S(1)}, u32[]{:S(2)}, u32[]{:S(2)}) collective-permute-start(f32[1,8,16,128]{3,1,2,0:T(8,128)S(1)} %get-tuple-element.116), channel_id=1, source_target_pairs={{1,0},{2,1},{3,2},{4,3},{5,4},{6,5},{7,6},{9,8},{10,9},{11,10},{12... | collective-permute-start | bytes 196616 | tf_op jit(solution)/shard_map/ppermute | solution.py:19
  289.8 8.6 %collective-permute-start.18 = (f32[1,8,16,128]{3,1,2,0:T(8,128)S(1)}, f32[1,8,16,128]{3,1,2,0:T(8,128)S(1)}, u32[]{:S(2)}, u32[]{:S(2)}) collective-permute-start(f32[1,8,16,128]{3,1,2,0:T(8,128)S(1)} %get-tuple-element.113), channel_id=1, source_target_pairs={{0,1},{1,2},{2,3},{3,4},{4,5},{5,6},{6,7},{8,9},{9,10},{10,11},{11... | collective-permute-start | bytes 196616 | tf_op jit(solution)/shard_map/ppermute | solution.py:16
  295.0 7.8 %collective-permute-start.19 = (f32[1,8,16,128]{3,1,2,0:T(8,128)S(1)}, f32[1,8,16,128]{3,1,2,0:T(8,128)S(1)}, u32[]{:S(2)}, u32[]{:S(2)}) collective-permute-start(f32[1,8,16,128]{3,1,2,0:T(8,128)S(1)} %get-tuple-element.114), channel_id=1, source_target_pairs={{1,0},{2,1},{3,2},{4,3},{5,4},{6,5},{7,6},{9,8},{10,9},{11,10},{12... | collective-permute-start | bytes 196616 | tf_op jit(solution)/shard_map/ppermute | solution.py:19
  325.4 8.6 %collective-permute-start.20 = (f32[1,8,16,128]{3,1,2,0:T(8,128)S(1)}, f32[1,8,16,128]{3,1,2,0:T(8,128)S(1)}, u32[]{:S(2)}, u32[]{:S(2)}) collective-permute-start(f32[1,8,16,128]{3,1,2,0:T(8,128)S(1)} %get-tuple-element.111), channel_id=1, source_target_pairs={{0,1},{1,2},{2,3},{3,4},{4,5},{5,6},{6,7},{8,9},{9,10},{10,11},{11... | collective-permute-start | bytes 196616 | tf_op jit(solution)/shard_map/ppermute | solution.py:16
  329.1 7.8 %collective-permute-start.21 = (f32[1,8,16,128]{3,1,2,0:T(8,128)S(1)}, f32[1,8,16,128]{3,1,2,0:T(8,128)S(1)}, u32[]{:S(2)}, u32[]{:S(2)}) collective-permute-start(f32[1,8,16,128]{3,1,2,0:T(8,128)S(1)} %get-tuple-element.112), channel_id=1, source_target_pairs={{1,0},{2,1},{3,2},{4,3},{5,4},{6,5},{7,6},{9,8},{10,9},{11,10},{12... | collective-permute-start | bytes 196616 | tf_op jit(solution)/shard_map/ppermute | solution.py:19
  344.0 62.1 %copy-start.48 = (f32[2,32,2,128]{3,1,2,0:T(8,128)S(1)}, f32[2,32,2,128]{3,1,2,0:T(8,128)}, u32[]{:S(2)}) copy-start(f32[2,32,2,128]{3,1,2,0:T(8,128)} %copy-done.47) | copy-start | bytes 196612
  344.8 66.6 %copy-start.21 = (bf16[16,33,4,128]{3,0,2,1:T(8,128)(2,1)S(1)}, bf16[16,33,4,128]{3,0,2,1:T(8,128)(2,1)}, u32[]{:S(2)}) copy-start(bf16[16,33,4,128]{3,0,2,1:T(8,128)(2,1)} %copy-done.20) | copy-start | bytes 1622020
  406.8 2.6 collective-permute-start.22
  408.1 3.1 collective-permute-start.23
  418.7 8.8 %collective-permute-start.24 = (bf16[2,1,4,128]{3,1,2,0:T(2,128)(2,1)S(1)}, bf16[2,1,4,128]{3,1,2,0:T(2,128)(2,1)S(1)}, u32[]{:S(2)}, u32[]{:S(2)}) collective-permute-start(bf16[2,1,4,128]{3,1,2,0:T(2,128)(2,1)S(1)} %get-tuple-element.155), channel_id=1, source_target_pairs={{0,1},{1,2},{2,3},{3,4},{4,5},{5,6},{6,7},{8,9},{9,10},{10,11},{11... | collective-permute-start | bytes 6152 | tf_op jit(solution)/shard_map/ppermute | solution.py:16
  423.3 7.0 %collective-permute-start.25 = (bf16[2,1,4,128]{3,1,2,0:T(2,128)(2,1)S(1)}, bf16[2,1,4,128]{3,1,2,0:T(2,128)(2,1)S(1)}, u32[]{:S(2)}, u32[]{:S(2)}) collective-permute-start(bf16[2,1,4,128]{3,1,2,0:T(2,128)(2,1)S(1)} %get-tuple-element.156), channel_id=1, source_target_pairs={{1,0},{2,1},{3,2},{4,3},{5,4},{6,5},{7,6},{9,8},{10,9},{11,10},{12... | collective-permute-start | bytes 6152 | tf_op jit(solution)/shard_map/ppermute | solution.py:19
  459.1 105.5 %collective-permute-start.26 = (bf16[16,32,1,128]{3,0,2,1:T(8,128)(2,1)S(1)}, bf16[16,32,1,128]{3,0,2,1:T(8,128)(2,1)S(1)}, u32[]{:S(2)}, u32[]{:S(2)}) collective-permute-start(bf16[16,32,1,128]{3,0,2,1:T(8,128)(2,1)S(1)} %get-tuple-element.109), channel_id=1, source_target_pairs={{0,8},{8,16},{16,24},{24,32},{32,40},{40,48},{48,56},{56,64},{64,7... | collective-permute-start | bytes 393224 | tf_op jit(solution)/shard_map/ppermute | solution.py:16
  460.4 104.2 %collective-permute-start.27 = (bf16[16,32,1,128]{3,0,2,1:T(8,128)(2,1)S(1)}, bf16[16,32,1,128]{3,0,2,1:T(8,128)(2,1)S(1)}, u32[]{:S(2)}, u32[]{:S(2)}) collective-permute-start(bf16[16,32,1,128]{3,0,2,1:T(8,128)(2,1)S(1)} %get-tuple-element.110), channel_id=1, source_target_pairs={{8,0},{16,8},{24,16},{32,24},{40,32},{48,40},{56,48},{64,56},{72,6... | collective-permute-start | bytes 393224 | tf_op jit(solution)/shard_map/ppermute | solution.py:19
  461.9 110.4 %copy-start.97 = (bf16[1,16,16]{2,1,0:T(8,128)(2,1)S(1)}, bf16[1,16,16]{2,1,0:T(8,128)(2,1)}, u32[]{:S(2)}) copy-start(bf16[1,16,16]{2,1,0:T(8,128)(2,1)} %copy-done.96) | copy-start | bytes 1540
  520.5 52.0 %copy-start.99 = (bf16[1,16,16]{2,1,0:T(8,128)(2,1)S(1)}, bf16[1,16,16]{2,1,0:T(8,128)(2,1)}, u32[]{:S(2)}) copy-start(bf16[1,16,16]{2,1,0:T(8,128)(2,1)} %copy-done.98) | copy-start | bytes 1540
  564.6 8.2 %collective-permute-start.29 = (bf16[16,1,4,128]{3,0,2,1:T(8,128)(2,1)S(1)}, bf16[16,1,4,128]{3,0,2,1:T(8,128)(2,1)S(1)}, u32[]{:S(2)}, u32[]{:S(2)}) collective-permute-start(bf16[16,1,4,128]{3,0,2,1:T(8,128)(2,1)S(1)} %get-tuple-element.94), channel_id=1, source_target_pairs={{1,0},{2,1},{3,2},{4,3},{5,4},{6,5},{7,6},{9,8},{10,9},{11,10},{12... | collective-permute-start | bytes 49160 | tf_op jit(solution)/shard_map/ppermute | solution.py:19
  567.2 8.9 %collective-permute-start.28 = (bf16[16,1,4,128]{3,0,2,1:T(8,128)(2,1)S(1)}, bf16[16,1,4,128]{3,0,2,1:T(8,128)(2,1)S(1)}, u32[]{:S(2)}, u32[]{:S(2)}) collective-permute-start(bf16[16,1,4,128]{3,0,2,1:T(8,128)(2,1)S(1)} %get-tuple-element.93), channel_id=1, source_target_pairs={{0,1},{1,2},{2,3},{3,4},{4,5},{5,6},{6,7},{8,9},{9,10},{10,11},{11... | collective-permute-start | bytes 49160 | tf_op jit(solution)/shard_map/ppermute | solution.py:16
  (116 other events, 499.7 us)
Sparse Core Ops, SparseCore 0:
  79.6 38.5 all-gather.1
  345.0 61.0 reduce-scatter.1
